TPU v7x, 128 devices: a whole 4x4x4 slice. The times are simulated.
128 devices in a mesh: row: 16 (over z, x), mp: 8 (over y, core).
Axes of the slice: x: 4, y: 4, z: 4, core: 2. Of those that a mesh axis runs over, the one named last changes fastest.
Arguments:
- token_ids: int32 [128, 128], P('row'), may hold values from 0 to 511
- set_lengths: int32 [128], P('row'), may hold values from 32 to 128
- live_counts: int32 [16], replicated, may hold values from 1 to 8, 64 in all
- embed_table: bfloat16 [512, 5120], replicated, may hold values from -3 to 3
- position_table: bfloat16 [128, 5120], replicated, may hold values from -3 to 3
- norm_gain: float32 [5120], replicated, may hold values from 0.1 to 1.9
- w_query: bfloat16 [5120, 5120], P('row', 'mp')
- w_key: bfloat16 [5120, 5120], P('row', 'mp')
- w_value: bfloat16 [5120, 5120], P('row', 'mp'), may hold values from -0.078125 to 0.078125
- w_out: bfloat16 [5120, 5120], P('mp', 'row'), may hold values from -0.078125 to 0.078125
Outputs:
- verified: bfloat16 [128, 128, 5120], P('row', None, 'mp')
Inputs may be any that keep to these rules, and one draw needn't show every extreme that they name: Owner group g has live_counts[g] live sets, its first slots; the counts sum to 64 and one group holds 8. `set_lengths`: positions at or past a set's length are padding.
All inputs are finite; a program needn't handle non-finite values.
Results may differ from a plain program's by a relative error of at most 0.017.
Values may be sent and summed in bfloat16 or wider, within the bound.
No kernel may reach another device: no remote copies, remote signals or barrier semaphores. Data moves between devices by JAX's collectives and lax.ppermute only.
A program may use at most 128 MiB of HBM per device.

v0:
```python
import jax
import jax.numpy as jnp
from jax import lax
from jax.sharding import PartitionSpec as P

DH = 128


def prepare(group_ids, embed_table, position_table, norm_gain):
    summed = (
        jnp.take(embed_table, group_ids, axis=0).astype(jnp.float32)
        + position_table.astype(jnp.float32)[None]
    )
    stored = lax.optimization_barrier(summed.astype(jnp.bfloat16))
    widened = stored.astype(jnp.float32)
    inverse = lax.rsqrt(jnp.mean(widened * widened, axis=-1, keepdims=True) + 1e-05)
    normed = (widened * inverse * norm_gain).astype(jnp.bfloat16)
    return (stored, normed)


def attend(query, keys, values, group_lengths):
    set_count = group_lengths.shape[0]
    seq_len = query.shape[0] // set_count
    q_four = query.reshape(set_count, seq_len, -1, DH)
    k_four = keys.reshape(set_count, seq_len, -1, DH)
    v_four = values.reshape(set_count, seq_len, -1, DH)
    scores = jnp.einsum(
        "sqhd,skhd->shqk", q_four, k_four, preferred_element_type=jnp.float32
    ) * DH ** (-0.5)
    valid = jnp.arange(seq_len)[None, :] < group_lengths[:, None]
    scores = jnp.where(valid[:, None, None, :], scores, -1e30)
    highest = jnp.max(scores, axis=-1, keepdims=True)
    expo = jnp.exp(scores - highest)
    weights = (expo / jnp.sum(expo, axis=-1, keepdims=True)).astype(jnp.bfloat16)
    mixed = jnp.einsum("shqk,skhd->sqhd", weights, v_four, preferred_element_type=jnp.float32)
    return mixed.astype(jnp.bfloat16).reshape(set_count * seq_len, -1)


def verify(
    group_ids,
    group_lengths,
    live,
    embed_table,
    position_table,
    norm_gain,
    w_query,
    w_key,
    w_value,
    w_out,
):
    set_count, seq_len = group_ids.shape
    stored, normed = prepare(group_ids, embed_table, position_table, norm_gain)
    flat = normed.reshape(set_count * seq_len, -1)
    query = jnp.dot(
        flat, lax.all_gather(w_query, "row", axis=0, tiled=True), preferred_element_type=jnp.float32
    )
    keys = jnp.dot(
        flat, lax.all_gather(w_key, "row", axis=0, tiled=True), preferred_element_type=jnp.float32
    )
    values = jnp.dot(
        flat, lax.all_gather(w_value, "row", axis=0, tiled=True), preferred_element_type=jnp.float32
    )
    mixed = attend(
        query.astype(jnp.bfloat16),
        keys.astype(jnp.bfloat16),
        values.astype(jnp.bfloat16),
        group_lengths,
    )
    partial_value = jnp.dot(
        mixed, lax.all_gather(w_out, "row", axis=1, tiled=True), preferred_element_type=jnp.float32
    )
    summed = lax.psum_scatter(
        partial_value.astype(jnp.bfloat16), "mp", scatter_dimension=1, tiled=True
    ).astype(jnp.float32)
    features = summed.shape[1]
    residual = lax.dynamic_slice_in_dim(
        stored.reshape(set_count * seq_len, -1), lax.axis_index("mp") * features, features, 1
    )
    valid = jnp.arange(seq_len)[None, :] < group_lengths[:, None]
    keep = (live[:, None] & valid).reshape(-1, 1).astype(jnp.float32)
    output = ((residual.astype(jnp.float32) + summed) * keep).astype(jnp.bfloat16)
    return output.reshape(set_count, seq_len, features)


def on_device(
    token_ids,
    set_lengths,
    live_counts,
    embed_table,
    position_table,
    norm_gain,
    w_query,
    w_key,
    w_value,
    w_out,
):
    slot_count, seq_len = token_ids.shape
    my_group = lax.axis_index("row")
    own_live = jnp.arange(slot_count) < live_counts[my_group]
    return verify(
        token_ids,
        set_lengths,
        own_live,
        embed_table,
        position_table,
        norm_gain,
        w_query,
        w_key,
        w_value,
        w_out,
    )


def solution(mesh):
    in_specs = (
        P("row", None),
        P("row"),
        P(),
        P(),
        P(),
        P(),
        P("row", "mp"),
        P("row", "mp"),
        P("row", "mp"),
        P("mp", "row"),
    )
    out_specs = P("row", None, "mp")
    return jax.shard_map(
        on_device, mesh=mesh, in_specs=in_specs, out_specs=out_specs, check_vma=False
    )
```

profile of v0, /device:TPU:8, one launch (start us, length us, event | category | flops | bytes accessed | tf_op | source)
XLA Modules:
  0.0 366.0 jit_solution(6773406523633156874)
XLA Ops:
  6.5 0.7 all-gather.7.cloned.1.call-update
  7.3 0.7 all-gather.9.cloned.1.call-update
  8.1 0.7 all-gather.5.cloned.1.call-update
  8.8 0.5 all-gather.11.cloned.1.call-update
  9.4 1.6 convert_element_type.57
  11.0 21.7 %gather_fusion = bf16[1024,5120]{1,0:T(8,128)(2,1)} fusion(bf16[512,5120]{1,0:T(8,128)(2,1)} %param.13, s32[1024]{0:T(1024)S(1)} %bitcast_clamp_fusion), kind=kCustom, calls=%fused_computation | custom fusion | bytes 20975616 | tf_op jit(solution)/shard_map/jit(_take)/gather | solution.py:11
  32.7 11.0 %add_convert_fusion = bf16[8,128,5120]{2,1,0:T(8,128)(2,1)} fusion(f32[128,5120]{1,0:T(8,128)S(1)} %convert_element_type.57, bf16[8,128,5120]{2,1,0:T(8,128)(2,1)} %bitcast.28, pred[8,128]{1,0:T(8,128)(4,1)S(1)} %compare_and_fusion), kind=kLoop, calls=%fused_computation.7 | loop fusion | flops 20971520 | bytes 23593984 | tf_op jit(solution)/shard_map/convert_element_type | solution.py:14
  43.7 0.6 dynamic_slice.7
  44.3 0.7 iota_compare_fusion.1
  45.1 6.2 %fusion.1 = f32[8,128]{1,0:T(8,128)S(1)} fusion(bf16[8,128,5120]{2,1,0:T(8,128)(2,1)} %add_convert_fusion), kind=kLoop, calls=%fused_computation.4 | loop fusion | flops 15727616 | bytes 10489856 | tf_op jit(solution)/shard_map/reduce_sum | solution.py:16
  51.3 0.8 copy-done
  52.1 5.9 %fusion.3 = bf16[8,128,5120]{2,1,0:T(8,128)(2,1)} fusion(bf16[8,128,5120]{2,1,0:T(8,128)(2,1)S(1)} %copy-done, f32[5120]{0:T(1024)S(1)} %copy-done.3, f32[8,128]{1,0:T(8,128)S(1)} %add_rsqrt_fusion), kind=kLoop, calls=%fused_computation.6 | loop fusion | flops 20971520 | bytes 20996096 | tf_op jit(solution)/shard_map/convert_element_type | solution.py:17
  58.0 16.3 %all-gather.7.cloned.1.call-done = bf16[5120,640]{1,0:T(8,128)(2,1)} async-done(((bf16[320,640]{1,0:T(8,128)(2,1)}), bf16[5120,640]{1,0:T(8,128)(2,1)}) %all-gather.7.cloned.1.call-update) | async-done | bytes 6553616 | tf_op jit(solution)/shard_map/all_gather | solution.py:55
  74.4 12.9 %convolution_convert_fusion.3 = bf16[1024,640]{1,0:T(8,128)(2,1)S(1)} fusion(bf16[1024,5120]{1,0:T(8,128)(2,1)} %bitcast.30, bf16[5120,640]{1,0:T(8,128)(2,1)} %all-gather.7.cloned.1.call-done), kind=kOutput, calls=%fused_computation.16 | convolution fusion | flops 6711541760 | bytes 18350080 | tf_op jit(solution)/shard_map/dot_general | solution.py:54
  87.3 1.5 reshape.103
  88.8 49.9 %all-gather.9.cloned.1.call-done = bf16[5120,640]{1,0:T(8,128)(2,1)} async-done(((bf16[320,640]{1,0:T(8,128)(2,1)}), bf16[5120,640]{1,0:T(8,128)(2,1)}) %all-gather.9.cloned.1.call-update) | async-done | bytes 6553616 | tf_op jit(solution)/shard_map/all_gather | solution.py:58
  138.6 12.9 %convolution_convert_fusion.2 = bf16[1024,640]{1,0:T(8,128)(2,1)S(1)} fusion(bf16[1024,5120]{1,0:T(8,128)(2,1)} %bitcast.31, bf16[5120,640]{1,0:T(8,128)(2,1)} %all-gather.9.cloned.1.call-done), kind=kOutput, calls=%fused_computation.15 | convolution fusion | flops 6711541760 | bytes 18350080 | tf_op jit(solution)/shard_map/dot_general | solution.py:57
  151.5 2.5 reshape.104
  154.0 48.9 %all-gather.5.cloned.1.call-done = bf16[5120,640]{1,0:T(8,128)(2,1)} async-done(((bf16[320,640]{1,0:T(8,128)(2,1)}), bf16[5120,640]{1,0:T(8,128)(2,1)}) %all-gather.5.cloned.1.call-update) | async-done | bytes 6553616 | tf_op jit(solution)/shard_map/all_gather | solution.py:61
  202.9 12.9 %convolution_convert_fusion.4 = bf16[1024,640]{1,0:T(8,128)(2,1)S(1)} fusion(bf16[1024,5120]{1,0:T(8,128)(2,1)} %bitcast.32, bf16[5120,640]{1,0:T(8,128)(2,1)} %all-gather.5.cloned.1.call-done), kind=kOutput, calls=%fused_computation.17 | convolution fusion | flops 6711541760 | bytes 18350080 | tf_op jit(solution)/shard_map/dot_general | solution.py:60
  215.9 2.5 reshape.102
  218.3 2.6 fusion.8
  221.0 1.5 copy-done.1
  222.5 0.8 fusion.23
  223.5 3.0 fusion.5
  226.6 0.9 copy.30
  227.4 39.7 %all-gather.11.cloned.1.call-done = bf16[640,5120]{0,1:T(8,128)(2,1)} async-done(((bf16[640,320]{0,1:T(8,128)(2,1)}), bf16[640,5120]{0,1:T(8,128)(2,1)}) %all-gather.11.cloned.1.call-update) | async-done | bytes 6553616 | tf_op jit(solution)/shard_map/all_gather | solution.py:70
  267.1 13.7 %convolution_convert_fusion = bf16[1024,5120]{1,0:T(8,128)(2,1)} fusion(bf16[640,5120]{0,1:T(8,128)(2,1)} %all-gather.11.cloned.1.call-done, bf16[80,8,8,128]{3,2,1,0:T(8,128)(2,1)S(1)} %bitcast.34), kind=kOutput, calls=%fused_computation.8 | convolution fusion | flops 6716129280 | bytes 18350080 | tf_op jit(solution)/shard_map/dot_general | solution.py:69
  280.8 14.4 %copy.38 = bf16[1024,5120]{0,1:T(8,128)(2,1)} copy(bf16[1024,5120]{1,0:T(8,128)(2,1)} %convolution_convert_fusion) | data formatting | bytes 20971520
  295.2 59.7 %reduce-scatter.4.cloned.1.call-done = bf16[640,1024]{1,0:T(8,128)(2,1)} async-done(((bf16[5120,1024]{1,0:T(8,128)(2,1)}), bf16[640,1024]{1,0:T(8,128)(2,1)}) %reduce-scatter.4.cloned.1.call-update) | async-done | bytes 1310736
  354.9 1.7 copy.39
  356.6 2.8 multiply_convert_fusion
  (22 shorter events, 0.5 us)
Async XLA Ops:
  6.5 67.8 %all-gather.7.cloned.1.call-start = ((), (), s32[]{:S(2)}) async-start(), calls=%async_computation.2 | async-start | bytes 6963200 | tf_op jit(solution)/shard_map/all_gather | solution.py:55
  7.3 3.7 %copy-start.4 = (s32[8,128]{1,0:T(8,128)S(1)}, s32[8,128]{1,0:T(8,128)}, u32[]{:S(2)}) copy-start(s32[8,128]{1,0:T(8,128)} %param.10) | copy-start | bytes 12292
  7.3 131.4 %all-gather.9.cloned.1.call-start = ((), (), s32[]{:S(2)}) async-start(), calls=%async_computation.3 | async-start | bytes 6963200 | tf_op jit(solution)/shard_map/all_gather | solution.py:58
  8.0 194.9 %all-gather.5.cloned.1.call-start = ((), (), s32[]{:S(2)}) async-start(), calls=%async_computation.1 | async-start | bytes 6963200 | tf_op jit(solution)/shard_map/all_gather | solution.py:61
  8.8 258.3 %all-gather.11.cloned.1.call-start = ((), (), s32[]{:S(2)}) async-start(), calls=%async_computation.4 | async-start | bytes 6963200 | tf_op jit(solution)/shard_map/all_gather | solution.py:70
  9.3 345.6 %reduce-scatter.4.cloned.1.call-start = ((), (), s32[]{:S(2)}) async-start(), calls=%async_computation.5 | async-start | bytes 11796480
  32.7 11.0 %copy-start.6 = (s32[16]{0:T(128)S(1)}, s32[16]{0:T(128)}, u32[]{:S(2)}) copy-start(s32[16]{0:T(128)} %param.12) | copy-start | bytes 196
  32.7 12.3 %copy-start.5 = (s32[8]{0:T(128)S(1)}, s32[8]{0:T(128)}, u32[]{:S(2)}) copy-start(s32[8]{0:T(128)} %param.11) | copy-start | bytes 100
  32.7 18.6 %copy-start.3 = (f32[5120]{0:T(1024)S(1)}, f32[5120]{0:T(1024)}, u32[]{:S(2)}) copy-start(f32[5120]{0:T(1024)} %param.15) | copy-start | bytes 61444
  45.1 7.1 %copy-start = (bf16[8,128,5120]{2,1,0:T(8,128)(2,1)S(1)}, bf16[8,128,5120]{2,1,0:T(8,128)(2,1)}, u32[]{:S(2)}) copy-start(bf16[8,128,5120]{2,1,0:T(8,128)(2,1)} %add_convert_fusion) | copy-start | bytes 31457284
  221.0 1.5 copy-start.1
  221.0 2.5 copy-start.2
Sparse Core Ops, SparseCore 0:
  9.5 64.8 all-gather.6
  76.5 62.1 all-gather.8
  140.8 62.1 all-gather.4
  204.9 62.1 all-gather.10
  295.3 59.5 reduce-scatter.3
where the time goes:
time: 370 us; the launch traced here: 366 us
  waiting for transfers between devices  217 us (59%)
  matrix products  58.1 us (16%)
  local copies, waits for them, and re-layouts  48.2 us (13%)
  other arithmetic  29.1 us (8%)
  between operations  13.3 us (4%)
    unnamed x6, waiting for transfers between devices  62.3 us
    all_gather x1, waiting for transfers between devices, verify(): lax.all_gather(w_key, 'row', axis=0, tiled=True)  49.9 us
    all_gather x1, waiting for transfers between devices, verify(): lax.all_gather(w_value, 'row', axis=0, tiled=True)  48.9 us
    all_gather x1, waiting for transfers between devices, verify(): lax.all_gather(w_out, 'row', axis=1, tiled=True)  39.7 us
    gather x1, local copies, waits for them, and re-layouts, prepare(): jnp.take(embed_table, group_ids, axis=0).astype(jnp.float32)  21.7 us
    unnamed x16, local copies, waits for them, and re-layouts  18.6 us
    all_gather x1, waiting for transfers between devices, verify(): lax.all_gather(w_query, 'row', axis=0, tiled=True)  16.3 us
    dot_general x1, matrix products, verify(): jnp.dot(mixed, lax.all_gather(w_out, 'row', axis=1, tiled=True), preferre...  13.7 us
  transfers between devices with their start and end apart: 5, of which 5 were waited for; matrix products, arithmetic and copies ran while one was open for 27% of the time, Pallas kernels for 0%

commit v1 on v0

v1 whole, which is shorter than its diff:
```python
import jax
import jax.numpy as jnp
from jax import lax
from jax.experimental import pallas as pl
from jax.experimental.pallas import tpu as pltpu
from jax.sharding import PartitionSpec as P

D = 5120
DH = 128
HEADS = 5
ROWS = 16
VOCAB = 512
SEQ = 128
SLOTS = 8
TABLE = VOCAB + SEQ
BLOCK = D // ROWS
FEATURES = 640
PART_A = 128
PART_B = BLOCK - PART_A
F32 = jnp.float32
BF16 = jnp.bfloat16
VMEM = 32 << 20


def mm(a, b, dims):
    return lax.dot_general(a, b, (dims, ((), ())), preferred_element_type=F32)


def table_kernel(e_ref, p_ref, w_ref, t_ref, r_ref, t_acc, g_acc, ee_acc, pp_acc):
    step = pl.program_id(0)

    @pl.when(step == 0)
    def _():
        t_acc[...] = jnp.zeros_like(t_acc)
        g_acc[...] = jnp.zeros_like(g_acc)
        ee_acc[...] = jnp.zeros_like(ee_acc)
        pp_acc[...] = jnp.zeros_like(pp_acc)

    e, p = e_ref[...], p_ref[...]
    w = w_ref[...].reshape(2 * BLOCK, DH)
    t_acc[:VOCAB] += mm(e, w, ((1,), (0,)))
    t_acc[VOCAB:] += mm(p, w, ((1,), (0,)))
    g_acc[...] += mm(e, p, ((1,), (1,)))
    pp_acc[...] += mm(p, p, ((1,), (1,)))
    wide = e.astype(F32)
    square = wide * wide
    folded = square[:, :128]
    for k in range(1, 2 * BLOCK // 128):
        folded += square[:, 128 * k : 128 * (k + 1)]
    ee_acc[...] += folded

    @pl.when(step == pl.num_programs(0) - 1)
    def _():
        t_ref[...] = t_acc[...].T.astype(BF16)
        ee = jnp.sum(ee_acc[...], axis=1, keepdims=True)
        diagonal = lax.broadcasted_iota(jnp.int32, (SEQ, SEQ), 0) == lax.broadcasted_iota(
            jnp.int32, (SEQ, SEQ), 1
        )
        pp = jnp.sum(jnp.where(diagonal, pp_acc[...], 0.0), axis=0, keepdims=True)
        total = jnp.maximum(ee + 2.0 * g_acc[...] + pp, 0.0)
        r_ref[...] = lax.rsqrt(total * (1.0 / D) + 1e-05)


def project_tables(embed_table, position_table, w_block):
    return pl.pallas_call(
        table_kernel,
        grid=(ROWS // 2,),
        in_specs=[
            pl.BlockSpec((VOCAB, 2 * BLOCK), lambda k: (0, k)),
            pl.BlockSpec((SEQ, 2 * BLOCK), lambda k: (0, k)),
            pl.BlockSpec((2, BLOCK, DH), lambda k: (k, 0, 0)),
        ],
        out_specs=[
            pl.BlockSpec((DH, TABLE), lambda k: (0, 0)),
            pl.BlockSpec((VOCAB, SEQ), lambda k: (0, 0)),
        ],
        out_shape=[
            jax.ShapeDtypeStruct((DH, TABLE), BF16),
            jax.ShapeDtypeStruct((VOCAB, SEQ), F32),
        ],
        scratch_shapes=[
            pltpu.VMEM((TABLE, DH), F32),
            pltpu.VMEM((VOCAB, SEQ), F32),
            pltpu.VMEM((VOCAB, 128), F32),
            pltpu.VMEM((SEQ, SEQ), F32),
        ],
        compiler_params=pltpu.CompilerParams(vmem_limit_bytes=VMEM),
        name="project_tables",
    )(embed_table, position_table, w_block)


def attend_kernel(lens_ref, live_ref, ids_ref, r_ref, t_ref, out_ref):
    step = pl.program_id(0)

    @pl.when(2 * step >= live_ref[0])
    def _():
        out_ref[...] = jnp.zeros_like(out_ref)

    @pl.when(2 * step < live_ref[0])
    def _():
        vocab = lax.broadcasted_iota(jnp.int32, (VOCAB, SEQ), 0)
        eye = lax.broadcasted_iota(jnp.int32, (SEQ, SEQ), 0) == lax.broadcasted_iota(
            jnp.int32, (SEQ, SEQ), 1
        )
        picks, scales = [], []
        for s in range(2):
            hit = vocab == ids_ref[pl.ds(2 * step + s, 1), :]
            scales.append(jnp.sum(jnp.where(hit, r_ref[...], 0.0), axis=0, keepdims=True))
            picks.append(
                jnp.concatenate(
                    [jnp.where(hit, 1.0, 0.0).astype(BF16), jnp.where(eye, 1.0, 0.0).astype(BF16)], 0
                )
            )
        pick = jnp.concatenate(picks, axis=1)
        scale = jnp.concatenate(scales, axis=1)
        table = t_ref[...].reshape(ROWS * DH, TABLE)
        rows = (mm(table[: 15 * DH], pick, ((1,), (0,))) * scale).astype(BF16)
        key_at = lax.broadcasted_iota(jnp.int32, (SEQ, SEQ), 0)
        for s in range(2):
            valid = key_at < lens_ref[2 * step + s]
            cols = slice(SEQ * s, SEQ * (s + 1))
            for h in range(HEADS):
                q = rows[DH * h : DH * (h + 1), cols]
                k = rows[DH * (HEADS + h) : DH * (HEADS + h + 1), cols]
                v = rows[DH * (2 * HEADS + h) : DH * (2 * HEADS + h + 1), cols]
                scores = mm(k, q, ((0,), (0,))) * DH ** (-0.5)
                scores = jnp.where(valid, scores, -1e30)
                expo = jnp.exp(scores - jnp.max(scores, axis=0, keepdims=True))
                weights = (expo / jnp.sum(expo, axis=0, keepdims=True)).astype(BF16)
                mixed = mm(v, weights, ((1,), (0,)))
                out_ref[cols, DH * h : DH * (h + 1)] = mixed.T.astype(BF16)


def attend(lengths, live, ids, r, tables):
    return pl.pallas_call(
        attend_kernel,
        grid_spec=pltpu.PrefetchScalarGridSpec(
            num_scalar_prefetch=2,
            grid=(SLOTS // 2,),
            in_specs=[
                pl.BlockSpec((SLOTS, SEQ), lambda i, *_: (0, 0)),
                pl.BlockSpec((VOCAB, SEQ), lambda i, *_: (0, 0)),
                pl.BlockSpec((ROWS, DH, TABLE), lambda i, *_: (0, 0, 0)),
            ],
            out_specs=pl.BlockSpec((2 * SEQ, FEATURES), lambda i, *_: (i, 0)),
        ),
        out_shape=jax.ShapeDtypeStruct((SLOTS * SEQ, FEATURES), BF16),
        compiler_params=pltpu.CompilerParams(vmem_limit_bytes=VMEM),
        name="attend",
    )(lengths, live, ids, r, tables)


def other_kernel(dest_ref, a_ref, w_ref, out_ref):
    w = w_ref[...].reshape(-1, FEATURES)
    out_ref[0] = mm(a_ref[...], w, ((1,), (1,))).astype(BF16)


def other_partials(dest, mixed, w):
    width = 2 * w.shape[1]
    tokens = mixed.shape[0]
    return pl.pallas_call(
        other_kernel,
        grid_spec=pltpu.PrefetchScalarGridSpec(
            num_scalar_prefetch=1,
            grid=(4,),
            in_specs=[
                pl.BlockSpec((tokens, FEATURES), lambda o, d: (0, 0)),
                pl.BlockSpec((2, width // 2, FEATURES), lambda o, d: (d[o], 0, 0)),
            ],
            out_specs=pl.BlockSpec((1, tokens, width), lambda o, d: (o, 0, 0)),
        ),
        out_shape=jax.ShapeDtypeStruct((4, tokens, width), BF16),
        compiler_params=pltpu.CompilerParams(vmem_limit_bytes=VMEM),
        name="other_partials",
    )(dest, mixed, w)


def own_kernel(dest_ref, a_ref, w0, w1, w2, w3, got_ref, *out_refs):
    for o, w_ref in enumerate((w0, w1, w2, w3)):
        w = w_ref[...].reshape(-1, FEATURES)
        part = mm(a_ref[...], w, ((1,), (1,))).astype(BF16).astype(F32)
        out_refs[o][...] = (part + got_ref[o].astype(F32)).astype(BF16)


def own_partials(dest, mixed, w, got):
    width = 2 * w.shape[1]
    tokens = mixed.shape[0]
    tile = 256

    def pick(o):
        return pl.BlockSpec((2, width // 2, FEATURES), lambda i, d: (d[o], 0, 0))

    return pl.pallas_call(
        own_kernel,
        grid_spec=pltpu.PrefetchScalarGridSpec(
            num_scalar_prefetch=1,
            grid=(tokens // tile,),
            in_specs=[
                pl.BlockSpec((tile, FEATURES), lambda i, d: (i, 0)),
                pick(0),
                pick(1),
                pick(2),
                pick(3),
                pl.BlockSpec((4, tile, width), lambda i, d: (0, i, 0)),
            ],
            out_specs=[pl.BlockSpec((tile, width), lambda i, d: (i, 0))] * 4,
        ),
        out_shape=[jax.ShapeDtypeStruct((tokens, width), BF16)] * 4,
        compiler_params=pltpu.CompilerParams(vmem_limit_bytes=VMEM),
        name="own_partials",
    )(dest, mixed, w, w, w, w, got)


def finish_kernel(lens_ref, live_ref, at_ref, ids_ref, e_ref, p_ref, *refs):
    a_refs, b_refs, out_ref = refs[:4], refs[4:8], refs[8]
    slot = pl.program_id(0)
    live = slot < live_ref[0]

    @pl.when(jnp.logical_not(live))
    def _():
        out_ref[...] = jnp.zeros_like(out_ref)

    @pl.when(live)
    def _():
        hit = lax.broadcasted_iota(jnp.int32, (VOCAB, SEQ), 0) == ids_ref[pl.ds(slot, 1), :]
        pick = jnp.where(hit, 1.0, 0.0).astype(BF16)
        stored = mm(pick, e_ref[...], ((0,), (0,))) + p_ref[...].astype(F32)
        stored = stored.astype(BF16).astype(F32)
        a = sum(ref[...].astype(F32) for ref in a_refs)
        b = sum(ref[...].astype(F32) for ref in b_refs)
        total = jnp.concatenate([a[:, :128], b[:, :256], a[:, 128:], b[:, 256:]], axis=1)
        valid = lax.broadcasted_iota(jnp.int32, (SEQ, FEATURES), 0) < lens_ref[slot]
        out_ref[0] = jnp.where(valid, stored + total, 0.0).astype(BF16)


def finish(lengths, live, at, ids, embed_table, position_table, a_parts, b_parts):
    part = [pl.BlockSpec((SEQ, x.shape[1]), lambda s, *_: (s, 0)) for x in (*a_parts, *b_parts)]
    return pl.pallas_call(
        finish_kernel,
        grid_spec=pltpu.PrefetchScalarGridSpec(
            num_scalar_prefetch=3,
            grid=(SLOTS,),
            in_specs=[
                pl.BlockSpec((SLOTS, SEQ), lambda s, *_: (0, 0)),
                pl.BlockSpec((VOCAB, FEATURES), lambda s, n, c, at: (0, at[0])),
                pl.BlockSpec((SEQ, FEATURES), lambda s, n, c, at: (0, at[0])),
                *part,
            ],
            out_specs=pl.BlockSpec((1, SEQ, FEATURES), lambda s, *_: (s, 0, 0)),
        ),
        out_shape=jax.ShapeDtypeStruct((SLOTS, SEQ, FEATURES), BF16),
        compiler_params=pltpu.CompilerParams(vmem_limit_bytes=VMEM),
        name="finish",
    )(lengths, live, at, ids, embed_table, position_table, *a_parts, *b_parts)


def on_device(
    token_ids,
    set_lengths,
    live_counts,
    embed_table,
    position_table,
    norm_gain,
    w_query,
    w_key,
    w_value,
    w_out,
):
    row = lax.axis_index("row")
    part = lax.axis_index("mp")
    y, core = part // 2, part % 2
    live = live_counts[row].reshape(1)

    turned = w_out.T
    odd = jnp.concatenate([turned[64:192], turned[:64], turned[192:]], axis=0)
    turned = jnp.where(row % 2 == 1, odd, turned)
    wa = lax.all_gather(turned[:PART_A], "row", axis=0)

    gain = lax.dynamic_slice_in_dim(norm_gain, row * BLOCK, BLOCK)[:, None]
    blocks = [
        (gain * w.astype(F32)).astype(BF16).reshape(BLOCK, HEADS, DH)
        for w in (w_query, w_key, w_value)
    ]
    packed = jnp.concatenate([*blocks, jnp.zeros((BLOCK, 1, DH), BF16)], axis=1)
    w_block = lax.all_to_all(packed.transpose(1, 0, 2), "row", 0, 0)

    mine, r = project_tables(embed_table, position_table, w_block)
    tables = lax.all_gather(mine, "row", axis=0)

    rest, tables = lax.optimization_barrier((turned[PART_A:], tables))
    wb = lax.all_gather(rest, "row", axis=0)

    mixed = attend(set_lengths, live, token_ids, r, tables)

    lines = (y + jnp.arange(4, dtype=jnp.int32)) % 4
    other = 2 * lines + 1 - core
    own = 2 * lines + core
    swap = [(2 * i + c, 2 * i + 1 - c) for i in range(4) for c in range(2)]

    def along(o):
        return [(2 * i + c, 2 * ((i + o) % 4) + c) for i in range(4) for c in range(2)]

    sums = []
    for w in (wa, wb):
        got = lax.ppermute(other_partials(other, mixed, w), "mp", swap)
        parts = own_partials(own, mixed, w, got)
        sums.append([parts[0]] + [lax.ppermute(parts[o], "mp", along(o)) for o in (1, 3, 2)])
    return finish(
        set_lengths,
        live,
        part.reshape(1),
        token_ids,
        embed_table,
        position_table,
        sums[0],
        sums[1],
    )


def solution(mesh):
    in_specs = (
        P("row", None),
        P("row"),
        P(),
        P(),
        P(),
        P(),
        P("row", "mp"),
        P("row", "mp"),
        P("row", "mp"),
        P("mp", "row"),
    )
    out_specs = P("row", None, "mp")
    return jax.shard_map(
        on_device, mesh=mesh, in_specs=in_specs, out_specs=out_specs, check_vma=False
    )
```

time: 370 us -> 284 us (0.77)
  matrix products: 58.1 us -> 0 us
  local copies, waits for them, and re-layouts: 48.2 us -> 12.6 us
  Pallas kernels: 0 us -> 32.8 us
  waiting for transfers between devices: 217 us -> 185 us
  blocking collectives: 0 us -> 27.8 us
  other arithmetic: 29.1 us -> 1.84 us
  starting transfers between devices: 0.15 us -> 9.19 us
    unnamed x6 -> x3, waiting for transfers between devices: 62.3 us -> 0.05 us
    dot_general x6 -> x0, matrix products: 58.1 us -> none  [the longest x1 13.7 us: verify(): jnp.dot(mixed, lax.all_gather(w_out, 'row', axis=1, tiled=True), preferre...]
    ppermute x0 -> x8, waiting for transfers between devices: none -> 56.7 us  [the longest x6 52.6 us: on_device(): lax.ppermute(parts[o], 'mp', along(o))]
    pallas_call x0 -> x7, Pallas kernels: none -> 32.8 us  [the longest x2 9.15 us: own_partials(): pl.pallas_call(own_kernel, grid_spec=pltpu.PrefetchScalarGridSpec(num_sca...]
    all_to_all x0 -> x1, blocking collectives: none -> 27.8 us  [on_device(): w_block = lax.all_to_all(packed.transpose(1, 0, 2), 'row', 0, 0)]
    all_gather x4 -> x3, waiting for transfers between devices: 155 us -> 128 us  [the longest x1 44.4 us: on_device(): wb = lax.all_gather(rest, 'row', axis=0)]
    gather x1 -> x0, local copies, waits for them, and re-layouts: 21.7 us -> none  [prepare(): jnp.take(embed_table, group_ids, axis=0).astype(jnp.float32)]
    convert_element_type x5 -> x1, other arithmetic: 21.3 us -> 1.52 us  [on_device(): (gain * w.astype(F32)).astype(BF16).reshape(BLOCK, HEADS, DH)]
  transfers between devices with their start and end apart: 5 -> 11, of which waited for: 5 -> 7; matrix products, arithmetic and copies ran while one was open for 27% -> 1% of each run, Pallas kernels for 0% -> 8%
where the time goes in v1:
time: 284 us; the launch traced here: 282 us
  waiting for transfers between devices  185 us (65%)
  Pallas kernels  32.8 us (12%)
  blocking collectives  27.8 us (10%)
  between operations  13.4 us (5%)
  local copies, waits for them, and re-layouts  12.6 us (4%)
  starting transfers between devices  9.19 us (3%)
    ppermute x6, waiting for transfers between devices, on_device(): lax.ppermute(parts[o], 'mp', along(o))  52.6 us
    all_gather x1, waiting for transfers between devices, on_device(): wb = lax.all_gather(rest, 'row', axis=0)  44.4 us
    all_gather x1, waiting for transfers between devices, on_device(): tables = lax.all_gather(mine, 'row', axis=0)  43.1 us
    all_gather x1, waiting for transfers between devices, on_device(): wa = lax.all_gather(turned[:PART_A], 'row', axis=0)  40.6 us
    all_to_all x1, blocking collectives, on_device(): w_block = lax.all_to_all(packed.transpose(1, 0, 2), 'row', 0, 0)  27.8 us
    pallas_call x2, Pallas kernels, own_partials(): pl.pallas_call(own_kernel, grid_spec=pltpu.PrefetchScalarGridSpec(num_sca...  9.15 us
    ppermute x6, starting transfers between devices, on_device(): lax.ppermute(parts[o], 'mp', along(o))  9.02 us
    pallas_call x2, Pallas kernels, other_partials(): pl.pallas_call(other_kernel, grid_spec=pltpu.PrefetchScalarGridSpec(num_s...  8.22 us
  transfers between devices with their start and end apart: 11, of which 7 were waited for; matrix products, arithmetic and copies ran while one was open for 1% of the time, Pallas kernels for 8%

profile of v1, /device:TPU:8, one launch (start us, length us, event | category | flops | bytes accessed | tf_op | source)
XLA Modules:
  0.0 282.3 jit_solution(16350092148175097849)
XLA Ops:
  6.5 0.8 dynamic_slice.7
  7.3 1.5 multiply_convert_fusion.2
  9.4 0.3 copy.12
  9.9 0.3 copy.13
  10.7 27.8 %all_to_all.5.w_ref = bf16[16,320,128]{2,1,0:T(8,128)(2,1)S(1)} all-to-all(bf16[16,320,128]{2,1,0:T(8,128)(2,1)S(1)} %maximum_bitcast_fusion), channel_id=1, replica_groups=mesh['row'=16,'mp'=8] {'row'}, dimensions={0} | all-to-all | bytes 2621440 | tf_op jit(solution)/shard_map/all_to_all | solution.py:285
  38.5 2.5 copy-done.4
  41.0 6.5 %project_tables.1 = (bf16[128,640]{1,0:T(8,128)(2,1)}, f32[512,128]{1,0:T(8,128)S(1)}) custom-call(bf16[512,5120]{1,0:T(8,128)(2,1)S(1)} %copy-done.4, bf16[128,5120]{1,0:T(8,128)(2,1)S(1)} %copy-done.5, bf16[16,320,128]{2,1,0:T(8,128)(2,1)S(1)} %all_to_all.5.w_ref), custom_call_target="tpu_custom_call" | custom-call | tf_op jit(solution)/shard_map/project_tables/pallas_call | solution.py:65
  47.8 0.7 slice.23
  48.6 43.1 %all-gather.7.cloned.1.call-done = bf16[2048,640]{1,0:T(8,128)(2,1)} async-done(((bf16[128,640]{1,0:T(8,128)(2,1)}), bf16[2048,640]{1,0:T(8,128)(2,1)}) %all-gather.7.cloned.1.call-update) | async-done | bytes 2621456 | tf_op jit(solution)/shard_map/all_gather | solution.py:288
  91.7 0.7 slice.24
  92.4 0.6 dynamic_slice.6.live_ref
  93.0 1.7 copy-done.6
  94.8 4.5 %attend.1.a_ref = bf16[1024,640]{1,0:T(8,128)(2,1)S(1)} custom-call(s32[8]{0:T(128)S(1)} %copy-done.8, s32[1]{0:T(128)} %dynamic_slice.6.live_ref, s32[8,128]{1,0:T(8,128)S(1)} %copy-done.7, f32[512,128]{1,0:T(8,128)S(1)} %get-tuple-element.17.r_ref, bf16[16,128,640]{2,1,0:T(8,128)(2,1)S(1)} %bitcast.24), custom_call_target="tpu_custom_call" | custom-call | tf_op jit(solution)/shard_map/attend/pallas_call | solution.py:135
  99.3 44.4 %all-gather.11.cloned.1.call-done = bf16[3072,640]{1,0:T(8,128)(2,1)} async-done(((bf16[192,640]{1,0:T(8,128)(2,1)}), bf16[3072,640]{1,0:T(8,128)(2,1)}) %all-gather.11.cloned.1.call-update) | async-done | bytes 3932176 | tf_op jit(solution)/shard_map/all_gather | solution.py:291
  143.7 2.1 copy-done
  145.8 5.2 %other_partials.3 = bf16[4,1024,384]{2,1,0:T(8,128)(2,1)} custom-call(s32[4]{0:T(128)S(1)} %add_subtract_fusion.dest_ref, bf16[1024,640]{1,0:T(8,128)(2,1)S(1)} %attend.1.a_ref, bf16[16,192,640]{2,1,0:T(8,128)(2,1)S(1)} %bitcast.12), custom_call_target="tpu_custom_call" | custom-call | tf_op jit(solution)/shard_map/other_partials/pallas_call | solution.py:161
  151.0 40.6 %all-gather.9.cloned.1.call-done = bf16[2048,640]{1,0:T(8,128)(2,1)} async-done(((bf16[128,640]{1,0:T(8,128)(2,1)}), bf16[2048,640]{1,0:T(8,128)(2,1)}) %all-gather.9.cloned.1.call-update) | async-done | bytes 2621456 | tf_op jit(solution)/shard_map/all_gather | solution.py:277
  191.6 1.7 copy-done.2
  193.4 3.0 %other_partials.2 = bf16[4,1024,256]{2,1,0:T(8,128)(2,1)S(1)} custom-call(s32[4]{0:T(128)S(1)} %add_subtract_fusion.dest_ref, bf16[1024,640]{1,0:T(8,128)(2,1)S(1)} %attend.1.a_ref, bf16[16,128,640]{2,1,0:T(8,128)(2,1)S(1)} %bitcast.17), custom_call_target="tpu_custom_call" | custom-call | tf_op jit(solution)/shard_map/other_partials/pallas_call | solution.py:161
  196.5 4.1 %collective-permute-done.got_ref = bf16[4,1024,256]{2,1,0:T(8,128)(2,1)S(1)} collective-permute-done((bf16[4,1024,256]{2,1,0:T(8,128)(2,1)S(1)}, bf16[4,1024,256]{2,1,0:T(8,128)(2,1)S(1)}, u32[]{:S(2)}, u32[]{:S(2)}) %collective-permute-start) | collective-permute-done | bytes 2097184 | tf_op jit(solution)/shard_map/ppermute | solution.py:305
  200.7 3.2 %own_partials.2 = (bf16[1024,256]{1,0:T(8,128)(2,1)S(1)}, bf16[1024,256]{1,0:T(8,128)(2,1)S(1)}, bf16[1024,256]{1,0:T(8,128)(2,1)S(1)}, bf16[1024,256]{1,0:T(8,128)(2,1)S(1)}) custom-call(s32[4]{0:T(128)S(1)} %broadcast_add_fusion.dest_ref, bf16[1024,640]{1,0:T(8,128)(2,1)S(1)} %attend.1.a_ref, bf16[16,128,640]{2,1,0:T(8,128)(2,1)S(1)} %bitcast.18, ...), custom_call_target="tpu_custom_call" | custom-call | tf_op jit(solution)/shard_map/own_partials/pallas_call | solution.py:193
  203.9 1.6 collective-permute-start.1
  205.5 5.9 %own_partials.3 = (bf16[1024,384]{1,0:T(8,128)(2,1)S(1)}, bf16[1024,384]{1,0:T(8,128)(2,1)S(1)}, bf16[1024,384]{1,0:T(8,128)(2,1)S(1)}, bf16[1024,384]{1,0:T(8,128)(2,1)S(1)}) custom-call(s32[4]{0:T(128)S(1)} %broadcast_add_fusion.dest_ref, bf16[1024,640]{1,0:T(8,128)(2,1)S(1)} %attend.1.a_ref, bf16[16,192,640]{2,1,0:T(8,128)(2,1)S(1)} %bitcast.13, ...), custom_call_target="tpu_custom_call" | custom-call | tf_op jit(solution)/shard_map/own_partials/pallas_call | solution.py:193
  211.4 1.3 collective-permute-start.5
  212.7 0.8 collective-permute-start.6
  213.5 1.5 collective-permute-start.7
  215.0 1.7 collective-permute-start.2
  216.8 2.0 collective-permute-done.1.refs_1_
  218.8 2.1 collective-permute-start.3
  220.9 40.0 %collective-permute-done.2.refs_2_ = bf16[1024,256]{1,0:T(8,128)(2,1)S(1)} collective-permute-done((bf16[1024,256]{1,0:T(8,128)(2,1)S(1)}, bf16[1024,256]{1,0:T(8,128)(2,1)S(1)}, u32[]{:S(2)}, u32[]{:S(2)}) %collective-permute-start.2) | collective-permute-done | bytes 524320 | tf_op jit(solution)/shard_map/ppermute | solution.py:307
  260.9 10.5 %collective-permute-done.3.refs_3_ = bf16[1024,256]{1,0:T(8,128)(2,1)S(1)} collective-permute-done((bf16[1024,256]{1,0:T(8,128)(2,1)S(1)}, bf16[1024,256]{1,0:T(8,128)(2,1)S(1)}, u32[]{:S(2)}, u32[]{:S(2)}) %collective-permute-start.3) | collective-permute-done | bytes 524320 | tf_op jit(solution)/shard_map/ppermute | solution.py:307
  271.5 4.3 %finish.1 = bf16[8,128,640]{2,1,0:T(8,128)(2,1)} custom-call(s32[8]{0:T(128)S(1)} %copy-done.8, s32[1]{0:T(128)} %dynamic_slice.6.live_ref, s32[1]{0:T(128)} %bitcast.at_ref, s32[8,128]{1,0:T(8,128)S(1)} %copy-done.7, bf16[512,5120]{1,0:T(8,128)(2,1)S(1)} %bitcast.23, bf16[128,5120]{1,0:T(8,128)(2,1)S(1)} %copy-done.5, ...), custom_call_target="tpu_custom_call" | custom-call | tf_op jit(solution)/shard_map/finish/pallas_call | solution.py:238
  (46 shorter events, 1.8 us)
Async XLA Ops:
  6.5 85.1 %all-gather.7.cloned.1.call-start = ((), (), s32[]{:S(2)}) async-start(), calls=%async_computation.1 | async-start | bytes 2785280 | tf_op jit(solution)/shard_map/all_gather | solution.py:288
  10.7 27.8 %copy-start.5 = (bf16[128,5120]{1,0:T(8,128)(2,1)S(1)}, bf16[128,5120]{1,0:T(8,128)(2,1)}, u32[]{:S(2)}) copy-start(bf16[128,5120]{1,0:T(8,128)(2,1)} %p_ref.3) | copy-start | bytes 3932164
  38.5 2.5 copy-start.4
  41.0 6.6 %copy-start.9 = (bf16[640,320]{0,1:T(8,128)(2,1)S(1)}, bf16[640,320]{0,1:T(8,128)(2,1)}, u32[]{:S(2)}) copy-start(bf16[640,320]{0,1:T(8,128)(2,1)} %param.19) | copy-start | bytes 1228804
  47.6 96.1 %all-gather.11.cloned.1.call-start = ((), (), s32[]{:S(2)}) async-start(), calls=%async_computation.3 | async-start | bytes 4177920 | tf_op jit(solution)/shard_map/all_gather | solution.py:291
  47.7 44.7 %copy-start.10 = (s32[16]{0:T(128)S(1)}, s32[16]{0:T(128)}, u32[]{:S(2)}) copy-start(s32[16]{0:T(128)} %param.12) | copy-start | bytes 196
  47.7 45.3 %copy-start.7 = (s32[8,128]{1,0:T(8,128)S(1)}, s32[8,128]{1,0:T(8,128)}, u32[]{:S(2)}) copy-start(s32[8,128]{1,0:T(8,128)} %ids_ref.3) | copy-start | bytes 12292
  47.7 45.3 %copy-start.8 = (s32[8]{0:T(128)S(1)}, s32[8]{0:T(128)}, u32[]{:S(2)}) copy-start(s32[8]{0:T(128)} %lens_ref.3) | copy-start | bytes 100
  91.6 100.0 %all-gather.9.cloned.1.call-start = ((), (), s32[]{:S(2)}) async-start(), calls=%async_computation.2 | async-start | bytes 2785280 | tf_op jit(solution)/shard_map/all_gather | solution.py:277
  93.0 1.7 copy-start.6
  143.7 2.1 copy-start
  151.0 54.5 %collective-permute-start.4 = (bf16[4,1024,384]{2,1,0:T(8,128)(2,1)}, bf16[4,1024,384]{2,1,0:T(8,128)(2,1)}, u32[]{:S(2)}, u32[]{:S(2)}) collective-permute-start(bf16[4,1024,384]{2,1,0:T(8,128)(2,1)} %other_partials.3), channel_id=1, source_target_pairs={{0,1},{1,0},{2,3},{3,2},{4,5},{5,4},{6,7},{7,6},{8,9},{9,8},{10,11... | collective-permute-start | bytes 9437192 | tf_op jit(solution)/shard_map/ppermute | solution.py:305
  191.6 1.7 copy-start.2
  193.4 7.3 %copy-start.3 = (bf16[2048,640]{1,0:T(8,128)(2,1)S(1)}, bf16[2048,640]{1,0:T(8,128)(2,1)}, u32[]{:S(2)}) copy-start(bf16[2048,640]{1,0:T(8,128)(2,1)} %all-gather.9.cloned.1.call-done) | copy-start | bytes 7864324
  196.4 4.2 %collective-permute-start = (bf16[4,1024,256]{2,1,0:T(8,128)(2,1)S(1)}, bf16[4,1024,256]{2,1,0:T(8,128)(2,1)S(1)}, u32[]{:S(2)}, u32[]{:S(2)}) collective-permute-start(bf16[4,1024,256]{2,1,0:T(8,128)(2,1)S(1)} %other_partials.2), channel_id=1, source_target_pairs={{0,1},{1,0},{2,3},{3,2},{4,5},{5,4},{6,7},{7,6},{8,9},{9,8},{10,11... | collective-permute-start | bytes 6291464 | tf_op jit(solution)/shard_map/ppermute | solution.py:305
  200.7 4.8 %copy-start.1 = (bf16[3072,640]{1,0:T(8,128)(2,1)S(1)}, bf16[3072,640]{1,0:T(8,128)(2,1)}, u32[]{:S(2)}) copy-start(bf16[3072,640]{1,0:T(8,128)(2,1)} %all-gather.11.cloned.1.call-done) | copy-start | bytes 11796484
  203.9 67.5 %slice-start = ((s8[5242880]{0:T(1024)(128)(4,1)}), s8[4194304]{0:T(1024)(128)(4,1)S(1)}, s32[]{:S(2)}) async-start(s8[5242880]{0:T(1024)(128)(4,1)} %bitcast.22), calls=%async_computation.4 | async-start | bytes 8388608
  203.9 67.5 %slice-start.1 = ((s8[5242880]{0:T(1024)(128)(4,1)}), s8[1048576]{0:T(1024)(128)(4,1)S(1)}, s32[]{:S(2)}) async-start(s8[5242880]{0:T(1024)(128)(4,1)} %bitcast.22), calls=%async_computation.5 | async-start | bytes 2097152
  203.9 14.8 %collective-permute-start.1 = (bf16[1024,256]{1,0:T(8,128)(2,1)S(1)}, bf16[1024,256]{1,0:T(8,128)(2,1)S(1)}, u32[]{:S(2)}, u32[]{:S(2)}) collective-permute-start(bf16[1024,256]{1,0:T(8,128)(2,1)S(1)} %get-tuple-element.21), channel_id=1, source_target_pairs={{0,2},{1,3},{2,4},{3,5},{4,6},{5,7},{6,0},{7,1},{8,10},{9,11},{10,... | collective-permute-start | bytes 1572872 | tf_op jit(solution)/shard_map/ppermute | solution.py:307
  211.4 60.0 %collective-permute-start.5 = (bf16[1024,384]{1,0:T(8,128)(2,1)S(1)}, bf16[1024,384]{1,0:T(8,128)(2,1)S(1)}, u32[]{:S(2)}, u32[]{:S(2)}) collective-permute-start(bf16[1024,384]{1,0:T(8,128)(2,1)S(1)} %get-tuple-element.26), channel_id=1, source_target_pairs={{0,2},{1,3},{2,4},{3,5},{4,6},{5,7},{6,0},{7,1},{8,10},{9,11},{10,... | collective-permute-start | bytes 2359304 | tf_op jit(solution)/shard_map/ppermute | solution.py:307
  212.7 58.8 %collective-permute-start.6 = (bf16[1024,384]{1,0:T(8,128)(2,1)S(1)}, bf16[1024,384]{1,0:T(8,128)(2,1)S(1)}, u32[]{:S(2)}, u32[]{:S(2)}) collective-permute-start(bf16[1024,384]{1,0:T(8,128)(2,1)S(1)} %get-tuple-element.27), channel_id=1, source_target_pairs={{0,6},{1,7},{2,0},{3,1},{4,2},{5,3},{6,4},{7,5},{8,14},{9,15},{10,... | collective-permute-start | bytes 2359304 | tf_op jit(solution)/shard_map/ppermute | solution.py:307
  213.5 57.9 %collective-permute-start.7 = (bf16[1024,384]{1,0:T(8,128)(2,1)S(1)}, bf16[1024,384]{1,0:T(8,128)(2,1)S(1)}, u32[]{:S(2)}, u32[]{:S(2)}) collective-permute-start(bf16[1024,384]{1,0:T(8,128)(2,1)S(1)} %get-tuple-element.28), channel_id=1, source_target_pairs={{0,4},{1,5},{2,6},{3,7},{4,0},{5,1},{6,2},{7,3},{8,12},{9,13},{10,... | collective-permute-start | bytes 2359304 | tf_op jit(solution)/shard_map/ppermute | solution.py:307
  215.0 45.8 %collective-permute-start.2 = (bf16[1024,256]{1,0:T(8,128)(2,1)S(1)}, bf16[1024,256]{1,0:T(8,128)(2,1)S(1)}, u32[]{:S(2)}, u32[]{:S(2)}) collective-permute-start(bf16[1024,256]{1,0:T(8,128)(2,1)S(1)} %get-tuple-element.22), channel_id=1, source_target_pairs={{0,6},{1,7},{2,0},{3,1},{4,2},{5,3},{6,4},{7,5},{8,14},{9,15},{10,... | collective-permute-start | bytes 1572872 | tf_op jit(solution)/shard_map/ppermute | solution.py:307
  218.8 52.6 %collective-permute-start.3 = (bf16[1024,256]{1,0:T(8,128)(2,1)S(1)}, bf16[1024,256]{1,0:T(8,128)(2,1)S(1)}, u32[]{:S(2)}, u32[]{:S(2)}) collective-permute-start(bf16[1024,256]{1,0:T(8,128)(2,1)S(1)} %get-tuple-element.23), channel_id=1, source_target_pairs={{0,4},{1,5},{2,6},{3,7},{4,0},{5,1},{6,2},{7,3},{8,12},{9,13},{10,... | collective-permute-start | bytes 1572872 | tf_op jit(solution)/shard_map/ppermute | solution.py:307
Sparse Core Ops, SparseCore 0:
  47.7 43.8 all-gather.6
  93.7 49.9 all-gather.10
  145.8 45.7 all-gather.8

commit v2 on v1

--- a/solution.py
+++ b/solution.py
@@ -15,8 +15,8 @@
 TABLE = VOCAB + SEQ
 BLOCK = D // ROWS
 FEATURES = 640
-PART_A = 128
-PART_B = BLOCK - PART_A
+HALF = DH // 2
+SIDE = 4
 F32 = jnp.float32
 BF16 = jnp.bfloat16
 VMEM = 32 << 20
@@ -89,8 +89,18 @@
     )(embed_table, position_table, w_block)
 
 
-def attend_kernel(lens_ref, live_ref, ids_ref, r_ref, t_ref, out_ref):
+def attend_kernel(lens_ref, live_ref, at_ref, ids_ref, r_ref, *refs):
+    a_refs, b_refs, out_ref, table_ref = refs[:SIDE], refs[SIDE : 2 * SIDE], refs[-2], refs[-1]
     step = pl.program_id(0)
+    z, x = at_ref[0] // SIDE, at_ref[0] % SIDE
+
+    @pl.when(step == 0)
+    def _():
+        for dz in range(SIDE):
+            for dx in range(SIDE):
+                source = SIDE * ((z + SIDE - dz) % SIDE) + (x + SIDE - dx) % SIDE
+                table_ref[pl.ds(source, 1), :HALF] = a_refs[dz][dx : dx + 1]
+                table_ref[pl.ds(source, 1), HALF:] = b_refs[dx][dz : dz + 1]
 
     @pl.when(2 * step >= live_ref[0])
     def _():
@@ -113,8 +123,8 @@
             )
         pick = jnp.concatenate(picks, axis=1)
         scale = jnp.concatenate(scales, axis=1)
-        table = t_ref[...].reshape(ROWS * DH, TABLE)
-        rows = (mm(table[: 15 * DH], pick, ((1,), (0,))) * scale).astype(BF16)
+        table = table_ref[: 3 * HEADS].reshape(3 * HEADS * DH, TABLE)
+        rows = (mm(table, pick, ((1,), (0,))) * scale).astype(BF16)
         key_at = lax.broadcasted_iota(jnp.int32, (SEQ, SEQ), 0)
         for s in range(2):
             valid = key_at < lens_ref[2 * step + s]
@@ -131,23 +141,25 @@
                 out_ref[cols, DH * h : DH * (h + 1)] = mixed.T.astype(BF16)
 
 
-def attend(lengths, live, ids, r, tables):
+def attend(lengths, live, at, ids, r, a_parts, b_parts):
+    quarter = pl.BlockSpec((SIDE, HALF, TABLE), lambda i, *_: (0, 0, 0))
     return pl.pallas_call(
         attend_kernel,
         grid_spec=pltpu.PrefetchScalarGridSpec(
-            num_scalar_prefetch=2,
+            num_scalar_prefetch=3,
             grid=(SLOTS // 2,),
             in_specs=[
                 pl.BlockSpec((SLOTS, SEQ), lambda i, *_: (0, 0)),
                 pl.BlockSpec((VOCAB, SEQ), lambda i, *_: (0, 0)),
-                pl.BlockSpec((ROWS, DH, TABLE), lambda i, *_: (0, 0, 0)),
+                *[quarter] * (2 * SIDE),
             ],
             out_specs=pl.BlockSpec((2 * SEQ, FEATURES), lambda i, *_: (i, 0)),
+            scratch_shapes=[pltpu.VMEM((ROWS, DH, TABLE), BF16)],
         ),
         out_shape=jax.ShapeDtypeStruct((SLOTS * SEQ, FEATURES), BF16),
         compiler_params=pltpu.CompilerParams(vmem_limit_bytes=VMEM),
         name="attend",
-    )(lengths, live, ids, r, tables)
+    )(lengths, live, at, ids, r, *a_parts, *b_parts)
 
 
 def other_kernel(dest_ref, a_ref, w_ref, out_ref):
@@ -175,44 +187,81 @@
     )(dest, mixed, w)
 
 
-def own_kernel(dest_ref, a_ref, w0, w1, w2, w3, got_ref, *out_refs):
-    for o, w_ref in enumerate((w0, w1, w2, w3)):
-        w = w_ref[...].reshape(-1, FEATURES)
-        part = mm(a_ref[...], w, ((1,), (1,))).astype(BF16).astype(F32)
-        out_refs[o][...] = (part + got_ref[o].astype(F32)).astype(BF16)
-
-
-def own_partials(dest, mixed, w, got):
-    width = 2 * w.shape[1]
-    tokens = mixed.shape[0]
-    tile = 256
-
-    def pick(o):
-        return pl.BlockSpec((2, width // 2, FEATURES), lambda i, d: (d[o], 0, 0))
-
-    return pl.pallas_call(
-        own_kernel,
+def far_kernel(dest_ref, a_ref, w_ref, got_ref, left_ref, right_ref):
+    part = mm(a_ref[...], w_ref[...].reshape(-1, FEATURES), ((1,), (1,))).astype(BF16).astype(F32)
+    total = (part + got_ref[0].astype(F32)).astype(BF16)
+    left_ref[...] = total[:, : FEATURES // 2 + 64]
+    right_ref[...] = total[:, FEATURES // 2 + 64 :]
+
+
+def far_partials(dest, mixed, w, got):
+    tokens, tile = mixed.shape[0], 256
+    widths = (FEATURES // 2 + 64, FEATURES // 2 - 64)
+    return pl.pallas_call(
+        far_kernel,
         grid_spec=pltpu.PrefetchScalarGridSpec(
             num_scalar_prefetch=1,
             grid=(tokens // tile,),
             in_specs=[
                 pl.BlockSpec((tile, FEATURES), lambda i, d: (i, 0)),
-                pick(0),
+                pl.BlockSpec((2, BLOCK, FEATURES), lambda i, d: (d[2], 0, 0)),
+                pl.BlockSpec((1, tile, FEATURES), lambda i, d: (2, i, 0)),
+            ],
+            out_specs=[pl.BlockSpec((tile, n), lambda i, d: (i, 0)) for n in widths],
+        ),
+        out_shape=[jax.ShapeDtypeStruct((tokens, n), BF16) for n in widths],
+        compiler_params=pltpu.CompilerParams(vmem_limit_bytes=VMEM),
+        name="far_partials",
+    )(dest, mixed, w, got)
+
+
+def near_kernel(dest_ref, a_ref, w_up, w_down, got_ref, got_down, from_below, from_above, up_ref, down_ref):
+    cut = from_below.shape[1]
+    up = mm(a_ref[...], w_up[...].reshape(-1, FEATURES), ((1,), (1,))).astype(BF16).astype(F32)
+    up += got_ref[0].astype(F32)
+    up_ref[:, :cut] = (up[:, :cut] + from_below[...].astype(F32)).astype(BF16)
+    up_ref[:, cut:] = up[:, cut:].astype(BF16)
+    down = mm(a_ref[...], w_down[...].reshape(-1, FEATURES), ((1,), (1,))).astype(BF16).astype(F32)
+    down += got_down[0].astype(F32)
+    down_ref[:, :cut] = down[:, :cut].astype(BF16)
+    down_ref[:, cut:] = (down[:, cut:] + from_above[...].astype(F32)).astype(BF16)
+
+
+def near_partials(dest, mixed, w, got, from_below, from_above):
+    tokens, tile = mixed.shape[0], 256
+
+    def pick(o):
+        return pl.BlockSpec((2, BLOCK, FEATURES), lambda i, d: (d[o], 0, 0))
+
+    def had(o):
+        return pl.BlockSpec((1, tile, FEATURES), lambda i, d: (o, i, 0))
+
+    def rows(n):
+        return pl.BlockSpec((tile, n), lambda i, d: (i, 0))
+
+    return pl.pallas_call(
+        near_kernel,
+        grid_spec=pltpu.PrefetchScalarGridSpec(
+            num_scalar_prefetch=1,
+            grid=(tokens // tile,),
+            in_specs=[
+                rows(FEATURES),
                 pick(1),
-                pick(2),
                 pick(3),
-                pl.BlockSpec((4, tile, width), lambda i, d: (0, i, 0)),
+                had(1),
+                had(3),
+                rows(from_below.shape[1]),
+                rows(from_above.shape[1]),
             ],
-            out_specs=[pl.BlockSpec((tile, width), lambda i, d: (i, 0))] * 4,
+            out_specs=[rows(FEATURES)] * 2,
         ),
-        out_shape=[jax.ShapeDtypeStruct((tokens, width), BF16)] * 4,
-        compiler_params=pltpu.CompilerParams(vmem_limit_bytes=VMEM),
-        name="own_partials",
-    )(dest, mixed, w, w, w, w, got)
-
-
-def finish_kernel(lens_ref, live_ref, at_ref, ids_ref, e_ref, p_ref, *refs):
-    a_refs, b_refs, out_ref = refs[:4], refs[4:8], refs[8]
+        out_shape=[jax.ShapeDtypeStruct((tokens, FEATURES), BF16)] * 2,
+        compiler_params=pltpu.CompilerParams(vmem_limit_bytes=VMEM),
+        name="near_partials",
+    )(dest, mixed, w, w, got, got, from_below, from_above)
+
+
+def finish_kernel(dest_ref, lens_ref, live_ref, at_ref, ids_ref, e_ref, p_ref, a_ref, w_ref, got_ref, below, above, out_ref):
     slot = pl.program_id(0)
     live = slot < live_ref[0]
 
@@ -226,32 +275,35 @@
         pick = jnp.where(hit, 1.0, 0.0).astype(BF16)
         stored = mm(pick, e_ref[...], ((0,), (0,))) + p_ref[...].astype(F32)
         stored = stored.astype(BF16).astype(F32)
-        a = sum(ref[...].astype(F32) for ref in a_refs)
-        b = sum(ref[...].astype(F32) for ref in b_refs)
-        total = jnp.concatenate([a[:, :128], b[:, :256], a[:, 128:], b[:, 256:]], axis=1)
+        part = mm(a_ref[...], w_ref[...].reshape(-1, FEATURES), ((1,), (1,))).astype(BF16).astype(F32)
+        total = part + got_ref[0].astype(F32) + below[...].astype(F32) + above[...].astype(F32)
         valid = lax.broadcasted_iota(jnp.int32, (SEQ, FEATURES), 0) < lens_ref[slot]
         out_ref[0] = jnp.where(valid, stored + total, 0.0).astype(BF16)
 
 
-def finish(lengths, live, at, ids, embed_table, position_table, a_parts, b_parts):
-    part = [pl.BlockSpec((SEQ, x.shape[1]), lambda s, *_: (s, 0)) for x in (*a_parts, *b_parts)]
+def finish(dest, lengths, live, at, ids, embed_table, position_table, mixed, w, got, below, above):
+    rows = pl.BlockSpec((SEQ, FEATURES), lambda s, *_: (s, 0))
     return pl.pallas_call(
         finish_kernel,
         grid_spec=pltpu.PrefetchScalarGridSpec(
-            num_scalar_prefetch=3,
+            num_scalar_prefetch=4,
             grid=(SLOTS,),
             in_specs=[
                 pl.BlockSpec((SLOTS, SEQ), lambda s, *_: (0, 0)),
-                pl.BlockSpec((VOCAB, FEATURES), lambda s, n, c, at: (0, at[0])),
-                pl.BlockSpec((SEQ, FEATURES), lambda s, n, c, at: (0, at[0])),
-                *part,
+                pl.BlockSpec((VOCAB, FEATURES), lambda s, d, n, c, at: (0, at[0])),
+                pl.BlockSpec((SEQ, FEATURES), lambda s, d, n, c, at: (0, at[0])),
+                rows,
+                pl.BlockSpec((2, BLOCK, FEATURES), lambda s, d, n, c, at: (d[0], 0, 0)),
+                pl.BlockSpec((1, SEQ, FEATURES), lambda s, *_: (0, s, 0)),
+                rows,
+                rows,
             ],
             out_specs=pl.BlockSpec((1, SEQ, FEATURES), lambda s, *_: (s, 0, 0)),
         ),
         out_shape=jax.ShapeDtypeStruct((SLOTS, SEQ, FEATURES), BF16),
         compiler_params=pltpu.CompilerParams(vmem_limit_bytes=VMEM),
         name="finish",
-    )(lengths, live, at, ids, embed_table, position_table, *a_parts, *b_parts)
+    )(dest, lengths, live, at, ids, embed_table, position_table, mixed, w, got, below, above)
 
 
 def on_device(
@@ -271,10 +323,7 @@
     y, core = part // 2, part % 2
     live = live_counts[row].reshape(1)
 
-    turned = w_out.T
-    odd = jnp.concatenate([turned[64:192], turned[:64], turned[192:]], axis=0)
-    turned = jnp.where(row % 2 == 1, odd, turned)
-    wa = lax.all_gather(turned[:PART_A], "row", axis=0)
+    w_all = lax.all_gather(w_out.T, "row", axis=0)
 
     gain = lax.dynamic_slice_in_dim(norm_gain, row * BLOCK, BLOCK)[:, None]
     blocks = [
@@ -285,35 +334,53 @@
     w_block = lax.all_to_all(packed.transpose(1, 0, 2), "row", 0, 0)
 
     mine, r = project_tables(embed_table, position_table, w_block)
-    tables = lax.all_gather(mine, "row", axis=0)
-
-    rest, tables = lax.optimization_barrier((turned[PART_A:], tables))
-    wb = lax.all_gather(rest, "row", axis=0)
-
-    mixed = attend(set_lengths, live, token_ids, r, tables)
-
-    lines = (y + jnp.arange(4, dtype=jnp.int32)) % 4
+
+    def shifted(o, along_x):
+        pairs = []
+        for z in range(SIDE):
+            for x in range(SIDE):
+                to = SIDE * z + (x + o) % SIDE if along_x else SIDE * ((z + o) % SIDE) + x
+                pairs.append((SIDE * z + x, to))
+        return pairs
+
+    def spread(value, along_x):
+        near = {o: lax.ppermute(value, "row", shifted(o, along_x)) for o in (1, 3, 2)}
+        return [value, near[1], near[2], near[3]]
+
+    a_line = jnp.stack(spread(mine[:HALF], True))
+    b_line = jnp.stack(spread(mine[HALF:], False))
+    a_parts, b_parts = spread(a_line, False), spread(b_line, True)
+
+    mixed = attend(set_lengths, live, row.reshape(1), token_ids, r, a_parts, b_parts)
+
+    lines = (y + jnp.arange(SIDE, dtype=jnp.int32)) % SIDE
     other = 2 * lines + 1 - core
     own = 2 * lines + core
-    swap = [(2 * i + c, 2 * i + 1 - c) for i in range(4) for c in range(2)]
+    swap = [(2 * i + c, 2 * i + 1 - c) for i in range(SIDE) for c in range(2)]
 
     def along(o):
-        return [(2 * i + c, 2 * ((i + o) % 4) + c) for i in range(4) for c in range(2)]
-
-    sums = []
-    for w in (wa, wb):
-        got = lax.ppermute(other_partials(other, mixed, w), "mp", swap)
-        parts = own_partials(own, mixed, w, got)
-        sums.append([parts[0]] + [lax.ppermute(parts[o], "mp", along(o)) for o in (1, 3, 2)])
+        return [(2 * i + c, 2 * ((i + o) % SIDE) + c) for i in range(SIDE) for c in range(2)]
+
+    got = lax.ppermute(other_partials(other, mixed, w_all), "mp", swap)
+    left, right = far_partials(own, mixed, w_all, got)
+    from_below = lax.ppermute(left, "mp", along(1))
+    from_above = lax.ppermute(right, "mp", along(3))
+    up, down = near_partials(own, mixed, w_all, got, from_below, from_above)
+    below = lax.ppermute(up, "mp", along(1))
+    above = lax.ppermute(down, "mp", along(3))
     return finish(
+        own,
         set_lengths,
         live,
         part.reshape(1),
         token_ids,
         embed_table,
         position_table,
-        sums[0],
-        sums[1],
+        mixed,
+        w_all,
+        got,
+        below,
+        above,
     )
 
 

time: 284 us -> 216 us (0.76)
  the two profiles are of different devices: /device:TPU:8 before, /device:TPU:32 now
where the time goes in v2:
time: 216 us; the launch traced here: 215 us
  waiting for transfers between devices  83.5 us (39%)
  Pallas kernels  40.5 us (19%)
  blocking collectives  31.7 us (15%)
  starting transfers between devices  24.7 us (11%)
  local copies, waits for them, and re-layouts  19.4 us (9%)
  between operations  13.6 us (6%)
    all_to_all x1, blocking collectives, on_device(): w_block = lax.all_to_all(packed.transpose(1, 0, 2), 'row', 0, 0)  31.7 us
    ppermute x12, waiting for transfers between devices, spread(): lax.ppermute(value, 'row', shifted(o, along_x))  28.2 us
    ppermute x1, waiting for transfers between devices, on_device(): below = lax.ppermute(up, 'mp', along(1))  28.2 us
    ppermute x12, starting transfers between devices, spread(): lax.ppermute(value, 'row', shifted(o, along_x))  17.8 us
    unnamed x42, local copies, waits for them, and re-layouts  16.4 us
    pallas_call x1, Pallas kernels, attend(): pl.pallas_call(attend_kernel, grid_spec=pltpu.PrefetchScalarGridSpec(num_...  15.3 us
    ppermute x1, waiting for transfers between devices, on_device(): from_above = lax.ppermute(right, 'mp', along(3))  11.9 us
    ppermute x1, waiting for transfers between devices, on_device(): got = lax.ppermute(other_partials(other, mixed, w_all), 'mp', swap)  8.63 us
  transfers between devices with their start and end apart: 18, of which 10 were waited for; matrix products, arithmetic and copies ran while one was open for 2% of the time, Pallas kernels for 10%

profile of v2, /device:TPU:32, one launch (start us, length us, event | category | flops | bytes accessed | tf_op | source)
XLA Modules:
  0.0 215.2 jit_solution(15653577549887753693)
XLA Ops:
  8.0 1.5 multiply_convert_fusion.2
  11.5 31.7 %all_to_all.5.w_ref = bf16[16,320,128]{2,1,0:T(8,128)(2,1)S(1)} all-to-all(bf16[16,320,128]{2,1,0:T(8,128)(2,1)S(1)} %maximum_bitcast_fusion), channel_id=1, replica_groups=mesh['row'=16,'mp'=8] {'row'}, dimensions={0} | all-to-all | bytes 2621440 | tf_op jit(solution)/shard_map/all_to_all | solution.py:334
  43.2 2.5 %copy-done.4 = bf16[512,5120]{1,0:T(8,128)(2,1)S(1)} copy-done((bf16[512,5120]{1,0:T(8,128)(2,1)S(1)}, bf16[512,5120]{1,0:T(8,128)(2,1)}, u32[]{:S(2)}) %copy-start.4) | copy-done | bytes 5242904
  45.7 5.9 %project_tables.1 = (bf16[128,640]{1,0:T(8,128)(2,1)S(1)}, f32[512,128]{1,0:T(8,128)S(1)}) custom-call(bf16[512,5120]{1,0:T(8,128)(2,1)S(1)} %copy-done.4, bf16[128,5120]{1,0:T(8,128)(2,1)S(1)} %copy-done.5, bf16[16,320,128]{2,1,0:T(8,128)(2,1)S(1)} %all_to_all.5.w_ref), custom_call_target="tpu_custom_call" | custom-call | tf_op jit(solution)/shard_map/project_tables/pallas_call | solution.py:65
  51.6 2.4 %collective-permute-start.1 = (bf16[64,640]{1,0:T(8,128)(2,1)S(1)}, bf16[64,640]{1,0:T(8,128)(2,1)S(1)}, u32[]{:S(2)}, u32[]{:S(2)}) collective-permute-start(bf16[64,640]{1,0:T(8,128)(2,1)S(1)} %get-tuple-element.20), channel_id=1, source_target_pairs={{0,16},{8,24},{16,0},{24,8},{32,48},{40,56},{48,32},{56,40},{64,80... | collective-permute-start | bytes 245768 | tf_op jit(solution)/shard_map/ppermute | solution.py:347
  54.4 2.9 %collective-permute-start.2 = (bf16[64,640]{1,0:T(8,128)(2,1)S(1)}, bf16[64,640]{1,0:T(8,128)(2,1)S(1)}, u32[]{:S(2)}, u32[]{:S(2)}) collective-permute-start(bf16[64,640]{1,0:T(8,128)(2,1)S(1)} %get-tuple-element.20), channel_id=1, source_target_pairs={{0,24},{8,0},{16,8},{24,16},{32,56},{40,32},{48,40},{56,48},{64,88... | collective-permute-start | bytes 245768 | tf_op jit(solution)/shard_map/ppermute | solution.py:347
  57.3 2.0 collective-permute-done.1
  59.3 2.3 %collective-permute-done = bf16[64,640]{1,0:T(8,128)(2,1)S(1)} collective-permute-done((bf16[64,640]{1,0:T(8,128)(2,1)S(1)}, bf16[64,640]{1,0:T(8,128)(2,1)S(1)}, u32[]{:S(2)}, u32[]{:S(2)}) %collective-permute-start) | collective-permute-done | bytes 81952 | tf_op jit(solution)/shard_map/ppermute | solution.py:347
  61.6 2.0 collective-permute-start.5
  64.3 1.9 collective-permute-start.6
  66.3 2.9 %collective-permute-start.4 = (bf16[4,64,640]{2,1,0:T(8,128)(2,1)S(1)}, bf16[4,64,640]{2,1,0:T(8,128)(2,1)S(1)}, u32[]{:S(2)}, u32[]{:S(2)}) collective-permute-start(bf16[4,64,640]{2,1,0:T(8,128)(2,1)S(1)} %pad_maximum_fusion.refs_0_), channel_id=1, source_target_pairs={{0,64},{8,72},{16,80},{24,88},{32,96},{40,104},{48,112},{56,120},{... | collective-permute-start | bytes 983048 | tf_op jit(solution)/shard_map/ppermute | solution.py:347
  69.2 14.1 %collective-permute-done.7 = bf16[64,640]{1,0:T(8,128)(2,1)S(1)} collective-permute-done((bf16[64,640]{1,0:T(8,128)(2,1)S(1)}, bf16[64,640]{1,0:T(8,128)(2,1)S(1)}, u32[]{:S(2)}, u32[]{:S(2)}) %collective-permute-start.7) | collective-permute-done | bytes 81952 | tf_op jit(solution)/shard_map/ppermute | solution.py:347
  83.3 2.4 %collective-permute-done.8 = bf16[64,640]{1,0:T(8,128)(2,1)S(1)} collective-permute-done((bf16[64,640]{1,0:T(8,128)(2,1)S(1)}, bf16[64,640]{1,0:T(8,128)(2,1)S(1)}, u32[]{:S(2)}, u32[]{:S(2)}) %collective-permute-start.8) | collective-permute-done | bytes 81952 | tf_op jit(solution)/shard_map/ppermute | solution.py:347
  85.8 2.6 %collective-permute-start.11 = (bf16[4,64,640]{2,1,0:T(8,128)(2,1)S(1)}, bf16[4,64,640]{2,1,0:T(8,128)(2,1)S(1)}, u32[]{:S(2)}, u32[]{:S(2)}) collective-permute-start(bf16[4,64,640]{2,1,0:T(8,128)(2,1)S(1)} %pad_maximum_fusion.1.refs_4_), channel_id=1, source_target_pairs={{0,24},{8,0},{16,8},{24,16},{32,56},{40,32},{48,40},{56,48},{64,88... | collective-permute-start | bytes 983048 | tf_op jit(solution)/shard_map/ppermute | solution.py:347
  89.8 1.3 collective-permute-start.9
  91.7 6.5 %collective-permute-done.4.refs_2_ = bf16[4,64,640]{2,1,0:T(8,128)(2,1)S(1)} collective-permute-done((bf16[4,64,640]{2,1,0:T(8,128)(2,1)S(1)}, bf16[4,64,640]{2,1,0:T(8,128)(2,1)S(1)}, u32[]{:S(2)}, u32[]{:S(2)}) %collective-permute-start.4) | collective-permute-done | bytes 327712 | tf_op jit(solution)/shard_map/ppermute | solution.py:347
  102.0 1.0 copy-done.7
  103.0 1.0 copy-done.9
  106.9 15.3 %attend.1.a_ref = bf16[1024,640]{1,0:T(8,128)(2,1)S(1)} custom-call(s32[8]{0:T(128)S(1)} %copy-done.17, s32[1]{0:T(128)} %dynamic_slice.6.live_ref, s32[1]{0:T(128)} %bitcast.1.at_ref, s32[8,128]{1,0:T(8,128)S(1)} %copy-done.16, f32[512,128]{1,0:T(8,128)S(1)} %get-tuple-element.11.r_ref, bf16[4,64,640]{2,1,0:T(8,128)(2,1)S(1)} %pad_maximum_fusion.refs_0_, ...), custom_call_target="tpu_custom_call" | custom-call | tf_op jit(solution)/shard_map/attend/pallas_call | solution.py:146
  122.2 2.9 %copy-done = bf16[5120,640]{1,0:T(8,128)(2,1)S(1)} copy-done((bf16[5120,640]{1,0:T(8,128)(2,1)S(1)}, bf16[5120,640]{1,0:T(8,128)(2,1)}, u32[]{:S(2)}) %copy-start) | copy-done | bytes 6553624
  125.1 6.0 %other_partials.1 = bf16[4,1024,640]{2,1,0:T(8,128)(2,1)S(1)} custom-call(s32[4]{0:T(128)S(1)} %add_subtract_fusion.dest_ref, bf16[1024,640]{1,0:T(8,128)(2,1)S(1)} %attend.1.a_ref, bf16[16,320,640]{2,1,0:T(8,128)(2,1)S(1)} %bitcast.20), custom_call_target="tpu_custom_call" | custom-call | tf_op jit(solution)/shard_map/other_partials/pallas_call | solution.py:173
  131.2 8.6 %collective-permute-done.12.got_ref.got_down = bf16[4,1024,640]{2,1,0:T(8,128)(2,1)S(1)} collective-permute-done((bf16[4,1024,640]{2,1,0:T(8,128)(2,1)S(1)}, bf16[4,1024,640]{2,1,0:T(8,128)(2,1)S(1)}, u32[]{:S(2)}, u32[]{:S(2)}) %collective-permute-start.12) | collective-permute-done | bytes 5242912 | tf_op jit(solution)/shard_map/ppermute | solution.py:364
  139.8 2.5 %far_partials.1 = (bf16[1024,384]{1,0:T(8,128)(2,1)S(1)}, bf16[1024,256]{1,0:T(8,128)(2,1)S(1)}) custom-call(s32[4]{0:T(128)S(1)} %broadcast_add_fusion.dest_ref, bf16[1024,640]{1,0:T(8,128)(2,1)S(1)} %attend.1.a_ref, bf16[16,320,640]{2,1,0:T(8,128)(2,1)S(1)} %bitcast.21, bf16[4,1024,640]{2,1,0:T(8,128)(2,1)S(1)} %collective-permute-done.12.got_ref.got_down), custom_call_target="tpu_custom_call" | custom-call | tf_op jit(solution)/shard_map/far_partials/pallas_call | solution.py:200
  142.3 1.7 collective-permute-start.13
  144.0 1.7 collective-permute-start.14
  145.8 11.9 %collective-permute-done.14.from_above = bf16[1024,256]{1,0:T(8,128)(2,1)S(1)} collective-permute-done((bf16[1024,256]{1,0:T(8,128)(2,1)S(1)}, bf16[1024,256]{1,0:T(8,128)(2,1)S(1)}, u32[]{:S(2)}, u32[]{:S(2)}) %collective-permute-start.14) | collective-permute-done | bytes 524320 | tf_op jit(solution)/shard_map/ppermute | solution.py:367
  157.7 5.8 %collective-permute-done.13.from_below = bf16[1024,384]{1,0:T(8,128)(2,1)S(1)} collective-permute-done((bf16[1024,384]{1,0:T(8,128)(2,1)S(1)}, bf16[1024,384]{1,0:T(8,128)(2,1)S(1)}, u32[]{:S(2)}, u32[]{:S(2)}) %collective-permute-start.13) | collective-permute-done | bytes 786464 | tf_op jit(solution)/shard_map/ppermute | solution.py:366
  163.5 4.0 %near_partials.1 = (bf16[1024,640]{1,0:T(8,128)(2,1)S(1)}, bf16[1024,640]{1,0:T(8,128)(2,1)S(1)}) custom-call(s32[4]{0:T(128)S(1)} %broadcast_add_fusion.dest_ref, bf16[1024,640]{1,0:T(8,128)(2,1)S(1)} %attend.1.a_ref, bf16[16,320,640]{2,1,0:T(8,128)(2,1)S(1)} %bitcast.22, bf16[16,320,640]{2,1,0:T(8,128)(2,1)S(1)} %bitcast.23, ...), custom_call_target="tpu_custom_call" | custom-call | tf_op jit(solution)/shard_map/near_partials/pallas_call | solution.py:242
  167.7 3.1 %collective-permute-start.16 = (bf16[1024,640]{1,0:T(8,128)(2,1)S(1)}, bf16[1024,640]{1,0:T(8,128)(2,1)S(1)}, u32[]{:S(2)}, u32[]{:S(2)}) collective-permute-start(bf16[1024,640]{1,0:T(8,128)(2,1)S(1)} %get-tuple-element.16), channel_id=1, source_target_pairs={{0,6},{1,7},{2,0},{3,1},{4,2},{5,3},{6,4},{7,5},{8,14},{9,15},{10,... | collective-permute-start | bytes 3932168 | tf_op jit(solution)/shard_map/ppermute | solution.py:370
  170.8 28.2 %collective-permute-done.15.below = bf16[1024,640]{1,0:T(8,128)(2,1)S(1)} collective-permute-done((bf16[1024,640]{1,0:T(8,128)(2,1)S(1)}, bf16[1024,640]{1,0:T(8,128)(2,1)S(1)}, u32[]{:S(2)}, u32[]{:S(2)}) %collective-permute-start.15) | collective-permute-done | bytes 1310752 | tf_op jit(solution)/shard_map/ppermute | solution.py:369
  199.0 2.5 %copy-done.3 = bf16[4,1024,640]{2,1,0:T(8,128)(2,1)S(1)} copy-done((bf16[4,1024,640]{2,1,0:T(8,128)(2,1)S(1)}, bf16[4,1024,640]{2,1,0:T(8,128)(2,1)}, u32[]{:S(2)}) %copy-start.3) | copy-done | bytes 5242904
  201.5 6.9 %finish.1 = bf16[8,128,640]{2,1,0:T(8,128)(2,1)} custom-call(s32[4]{0:T(128)S(1)} %broadcast_add_fusion.dest_ref, s32[8]{0:T(128)S(1)} %copy-done.17, s32[1]{0:T(128)} %dynamic_slice.6.live_ref, s32[1]{0:T(128)} %bitcast.at_ref, s32[8,128]{1,0:T(8,128)S(1)} %copy-done.16, bf16[512,5120]{1,0:T(8,128)(2,1)S(1)} %bitcast.26, bf16[128,5120]{1,0:T(8,128)(2,1)S(1)} %copy-done.5, ...), custom_call_target="tpu_custom_call" | custom-call | tf_op jit(solution)/shard_map/finish/pallas_call | solution.py:286
  (71 shorter events, 13.7 us)
Async XLA Ops:
  6.5 115.7 %all-gather.3.cloned.1.call-start = ((), (), s32[]{:S(2)}) async-start(), calls=%async_computation.1 | async-start | bytes 6963200 | tf_op jit(solution)/shard_map/all_gather | solution.py:326
  11.5 31.7 %copy-start.5 = (bf16[128,5120]{1,0:T(8,128)(2,1)S(1)}, bf16[128,5120]{1,0:T(8,128)(2,1)}, u32[]{:S(2)}) copy-start(bf16[128,5120]{1,0:T(8,128)(2,1)} %p_ref.3) | copy-start | bytes 3932164
  43.2 2.5 %copy-start.4 = (bf16[512,5120]{1,0:T(8,128)(2,1)S(1)}, bf16[512,5120]{1,0:T(8,128)(2,1)}, u32[]{:S(2)}) copy-start(bf16[512,5120]{1,0:T(8,128)(2,1)} %e_ref.3) | copy-start | bytes 15728644
  51.6 39.6 %copy-start.18 = (s32[16]{0:T(128)S(1)}, s32[16]{0:T(128)}, u32[]{:S(2)}) copy-start(s32[16]{0:T(128)} %param.12) | copy-start | bytes 196
  51.6 50.4 %copy-start.16 = (s32[8,128]{1,0:T(8,128)S(1)}, s32[8,128]{1,0:T(8,128)}, u32[]{:S(2)}) copy-start(s32[8,128]{1,0:T(8,128)} %ids_ref.3) | copy-start | bytes 12292
  51.6 50.4 %copy-start.17 = (s32[8]{0:T(128)S(1)}, s32[8]{0:T(128)}, u32[]{:S(2)}) copy-start(s32[8]{0:T(128)} %lens_ref.3) | copy-start | bytes 100
  51.6 7.7 %collective-permute-start.1 = (bf16[64,640]{1,0:T(8,128)(2,1)S(1)}, bf16[64,640]{1,0:T(8,128)(2,1)S(1)}, u32[]{:S(2)}, u32[]{:S(2)}) collective-permute-start(bf16[64,640]{1,0:T(8,128)(2,1)S(1)} %get-tuple-element.20), channel_id=1, source_target_pairs={{0,16},{8,24},{16,0},{24,8},{32,48},{40,56},{48,32},{56,40},{64,80... | collective-permute-start | bytes 245768 | tf_op jit(solution)/shard_map/ppermute | solution.py:347
  54.0 7.5 %collective-permute-start = (bf16[64,640]{1,0:T(8,128)(2,1)S(1)}, bf16[64,640]{1,0:T(8,128)(2,1)S(1)}, u32[]{:S(2)}, u32[]{:S(2)}) collective-permute-start(bf16[64,640]{1,0:T(8,128)(2,1)S(1)} %get-tuple-element.20), channel_id=1, source_target_pairs={{0,8},{8,16},{16,24},{24,0},{32,40},{40,48},{48,56},{56,32},{64,72... | collective-permute-start | bytes 245768 | tf_op jit(solution)/shard_map/ppermute | solution.py:347
  54.4 7.2 %collective-permute-start.2 = (bf16[64,640]{1,0:T(8,128)(2,1)S(1)}, bf16[64,640]{1,0:T(8,128)(2,1)S(1)}, u32[]{:S(2)}, u32[]{:S(2)}) collective-permute-start(bf16[64,640]{1,0:T(8,128)(2,1)S(1)} %get-tuple-element.20), channel_id=1, source_target_pairs={{0,24},{8,0},{16,8},{24,16},{32,56},{40,32},{48,40},{56,48},{64,88... | collective-permute-start | bytes 245768 | tf_op jit(solution)/shard_map/ppermute | solution.py:347
  61.6 27.5 %collective-permute-start.5 = (bf16[4,64,640]{2,1,0:T(8,128)(2,1)S(1)}, bf16[4,64,640]{2,1,0:T(8,128)(2,1)S(1)}, u32[]{:S(2)}, u32[]{:S(2)}) collective-permute-start(bf16[4,64,640]{2,1,0:T(8,128)(2,1)S(1)} %pad_maximum_fusion.refs_0_), channel_id=1, source_target_pairs={{0,96},{8,104},{16,112},{24,120},{32,0},{40,8},{48,16},{56,24},{64... | collective-permute-start | bytes 983048 | tf_op jit(solution)/shard_map/ppermute | solution.py:347
  63.6 19.7 %collective-permute-start.7 = (bf16[64,640]{1,0:T(8,128)(2,1)S(1)}, bf16[64,640]{1,0:T(8,128)(2,1)S(1)}, u32[]{:S(2)}, u32[]{:S(2)}) collective-permute-start(bf16[64,640]{1,0:T(8,128)(2,1)S(1)} %get-tuple-element.19), channel_id=1, source_target_pairs={{0,64},{8,72},{16,80},{24,88},{32,96},{40,104},{48,112},{56,120},{... | collective-permute-start | bytes 245768 | tf_op jit(solution)/shard_map/ppermute | solution.py:347
  64.3 19.0 %collective-permute-start.6 = (bf16[64,640]{1,0:T(8,128)(2,1)S(1)}, bf16[64,640]{1,0:T(8,128)(2,1)S(1)}, u32[]{:S(2)}, u32[]{:S(2)}) collective-permute-start(bf16[64,640]{1,0:T(8,128)(2,1)S(1)} %get-tuple-element.19), channel_id=1, source_target_pairs={{0,32},{8,40},{16,48},{24,56},{32,64},{40,72},{48,80},{56,88},{64,... | collective-permute-start | bytes 245768 | tf_op jit(solution)/shard_map/ppermute | solution.py:347
  66.1 19.6 %collective-permute-start.8 = (bf16[64,640]{1,0:T(8,128)(2,1)S(1)}, bf16[64,640]{1,0:T(8,128)(2,1)S(1)}, u32[]{:S(2)}, u32[]{:S(2)}) collective-permute-start(bf16[64,640]{1,0:T(8,128)(2,1)S(1)} %get-tuple-element.19), channel_id=1, source_target_pairs={{0,96},{8,104},{16,112},{24,120},{32,0},{40,8},{48,16},{56,24},{64... | collective-permute-start | bytes 245768 | tf_op jit(solution)/shard_map/ppermute | solution.py:347
  66.3 31.9 %collective-permute-start.4 = (bf16[4,64,640]{2,1,0:T(8,128)(2,1)S(1)}, bf16[4,64,640]{2,1,0:T(8,128)(2,1)S(1)}, u32[]{:S(2)}, u32[]{:S(2)}) collective-permute-start(bf16[4,64,640]{2,1,0:T(8,128)(2,1)S(1)} %pad_maximum_fusion.refs_0_), channel_id=1, source_target_pairs={{0,64},{8,72},{16,80},{24,88},{32,96},{40,104},{48,112},{56,120},{... | collective-permute-start | bytes 983048 | tf_op jit(solution)/shard_map/ppermute | solution.py:347
  83.3 15.7 %collective-permute-start.3 = (bf16[4,64,640]{2,1,0:T(8,128)(2,1)S(1)}, bf16[4,64,640]{2,1,0:T(8,128)(2,1)S(1)}, u32[]{:S(2)}, u32[]{:S(2)}) collective-permute-start(bf16[4,64,640]{2,1,0:T(8,128)(2,1)S(1)} %pad_maximum_fusion.refs_0_), channel_id=1, source_target_pairs={{0,32},{8,40},{16,48},{24,56},{32,64},{40,72},{48,80},{56,88},{64,... | collective-permute-start | bytes 983048 | tf_op jit(solution)/shard_map/ppermute | solution.py:347
  85.8 13.9 %collective-permute-start.11 = (bf16[4,64,640]{2,1,0:T(8,128)(2,1)S(1)}, bf16[4,64,640]{2,1,0:T(8,128)(2,1)S(1)}, u32[]{:S(2)}, u32[]{:S(2)}) collective-permute-start(bf16[4,64,640]{2,1,0:T(8,128)(2,1)S(1)} %pad_maximum_fusion.1.refs_4_), channel_id=1, source_target_pairs={{0,24},{8,0},{16,8},{24,16},{32,56},{40,32},{48,40},{56,48},{64,88... | collective-permute-start | bytes 983048 | tf_op jit(solution)/shard_map/ppermute | solution.py:347
  88.4 12.0 %collective-permute-start.10 = (bf16[4,64,640]{2,1,0:T(8,128)(2,1)S(1)}, bf16[4,64,640]{2,1,0:T(8,128)(2,1)S(1)}, u32[]{:S(2)}, u32[]{:S(2)}) collective-permute-start(bf16[4,64,640]{2,1,0:T(8,128)(2,1)S(1)} %pad_maximum_fusion.1.refs_4_), channel_id=1, source_target_pairs={{0,16},{8,24},{16,0},{24,8},{32,48},{40,56},{48,32},{56,40},{64,80... | collective-permute-start | bytes 983048 | tf_op jit(solution)/shard_map/ppermute | solution.py:347
  89.8 12.2 %collective-permute-start.9 = (bf16[4,64,640]{2,1,0:T(8,128)(2,1)S(1)}, bf16[4,64,640]{2,1,0:T(8,128)(2,1)}, u32[]{:S(2)}, u32[]{:S(2)}) collective-permute-start(bf16[4,64,640]{2,1,0:T(8,128)(2,1)S(1)} %pad_maximum_fusion.1.refs_4_), channel_id=1, source_target_pairs={{0,8},{8,16},{16,24},{24,0},{32,40},{40,48},{48,56},{56,32},{64,72... | collective-permute-start | bytes 983048 | tf_op jit(solution)/shard_map/ppermute | solution.py:347
  102.0 1.0 copy-start.7
  103.0 1.0 copy-start.9
  104.0 1.0 copy-start.11
  122.2 2.9 %copy-start = (bf16[5120,640]{1,0:T(8,128)(2,1)S(1)}, bf16[5120,640]{1,0:T(8,128)(2,1)}, u32[]{:S(2)}) copy-start(bf16[5120,640]{1,0:T(8,128)(2,1)} %all-gather.3.cloned.1.call-done) | copy-start | bytes 19660804
  125.1 14.7 %copy-start.1 = (bf16[5120,640]{1,0:T(8,128)(2,1)S(1)}, bf16[5120,640]{1,0:T(8,128)(2,1)}, u32[]{:S(2)}) copy-start(bf16[5120,640]{1,0:T(8,128)(2,1)} %all-gather.3.cloned.1.call-done) | copy-start | bytes 19660804
  131.0 8.7 %collective-permute-start.12 = (bf16[4,1024,640]{2,1,0:T(8,128)(2,1)S(1)}, bf16[4,1024,640]{2,1,0:T(8,128)(2,1)S(1)}, u32[]{:S(2)}, u32[]{:S(2)}) collective-permute-start(bf16[4,1024,640]{2,1,0:T(8,128)(2,1)S(1)} %other_partials.1), channel_id=1, source_target_pairs={{0,1},{1,0},{2,3},{3,2},{4,5},{5,4},{6,7},{7,6},{8,9},{9,8},{10,11... | collective-permute-start | bytes 15728648 | tf_op jit(solution)/shard_map/ppermute | solution.py:364
  139.8 23.7 %copy-start.2 = (bf16[4,1024,640]{2,1,0:T(8,128)(2,1)}, bf16[4,1024,640]{2,1,0:T(8,128)(2,1)S(1)}, u32[]{:S(2)}) copy-start(bf16[4,1024,640]{2,1,0:T(8,128)(2,1)S(1)} %collective-permute-done.12.got_ref.got_down) | copy-start | bytes 15728644
  142.3 21.2 %collective-permute-start.13 = (bf16[1024,384]{1,0:T(8,128)(2,1)S(1)}, bf16[1024,384]{1,0:T(8,128)(2,1)S(1)}, u32[]{:S(2)}, u32[]{:S(2)}) collective-permute-start(bf16[1024,384]{1,0:T(8,128)(2,1)S(1)} %get-tuple-element.13), channel_id=1, source_target_pairs={{0,2},{1,3},{2,4},{3,5},{4,6},{5,7},{6,0},{7,1},{8,10},{9,11},{10,... | collective-permute-start | bytes 2359304 | tf_op jit(solution)/shard_map/ppermute | solution.py:366
  144.0 55.0 %slice-start = ((s8[5242880]{0:T(1024)(128)(4,1)}), s8[4194304]{0:T(1024)(128)(4,1)S(1)}, s32[]{:S(2)}) async-start(s8[5242880]{0:T(1024)(128)(4,1)} %bitcast.25), calls=%async_computation.2 | async-start | bytes 8388608
  144.0 55.0 %slice-start.1 = ((s8[5242880]{0:T(1024)(128)(4,1)}), s8[1048576]{0:T(1024)(128)(4,1)S(1)}, s32[]{:S(2)}) async-start(s8[5242880]{0:T(1024)(128)(4,1)} %bitcast.25), calls=%async_computation.3 | async-start | bytes 2097152
  144.0 13.7 %collective-permute-start.14 = (bf16[1024,256]{1,0:T(8,128)(2,1)S(1)}, bf16[1024,256]{1,0:T(8,128)(2,1)S(1)}, u32[]{:S(2)}, u32[]{:S(2)}) collective-permute-start(bf16[1024,256]{1,0:T(8,128)(2,1)S(1)} %get-tuple-element.14), channel_id=1, source_target_pairs={{0,6},{1,7},{2,0},{3,1},{4,2},{5,3},{6,4},{7,5},{8,14},{9,15},{10,... | collective-permute-start | bytes 1572872 | tf_op jit(solution)/shard_map/ppermute | solution.py:367
  167.5 31.5 %collective-permute-start.15 = (bf16[1024,640]{1,0:T(8,128)(2,1)S(1)}, bf16[1024,640]{1,0:T(8,128)(2,1)S(1)}, u32[]{:S(2)}, u32[]{:S(2)}) collective-permute-start(bf16[1024,640]{1,0:T(8,128)(2,1)S(1)} %get-tuple-element.15), channel_id=1, source_target_pairs={{0,2},{1,3},{2,4},{3,5},{4,6},{5,7},{6,0},{7,1},{8,10},{9,11},{10,... | collective-permute-start | bytes 3932168 | tf_op jit(solution)/shard_map/ppermute | solution.py:369
  167.7 31.3 %collective-permute-start.16 = (bf16[1024,640]{1,0:T(8,128)(2,1)S(1)}, bf16[1024,640]{1,0:T(8,128)(2,1)S(1)}, u32[]{:S(2)}, u32[]{:S(2)}) collective-permute-start(bf16[1024,640]{1,0:T(8,128)(2,1)S(1)} %get-tuple-element.16), channel_id=1, source_target_pairs={{0,6},{1,7},{2,0},{3,1},{4,2},{5,3},{6,4},{7,5},{8,14},{9,15},{10,... | collective-permute-start | bytes 3932168 | tf_op jit(solution)/shard_map/ppermute | solution.py:370
  199.0 2.5 %copy-start.3 = (bf16[4,1024,640]{2,1,0:T(8,128)(2,1)S(1)}, bf16[4,1024,640]{2,1,0:T(8,128)(2,1)}, u32[]{:S(2)}) copy-start(bf16[4,1024,640]{2,1,0:T(8,128)(2,1)} %copy-done.2) | copy-start | bytes 15728644
  (7 other events, 5.6 us)
Sparse Core Ops, SparseCore 0:
  9.5 87.4 all-gather.2
